TPU v7x, 512 devices: a whole 4x4x16 slice. The times are simulated.
512 devices in a mesh: dp: 128 (over y, z, core), tensor: 4 (over x).
Axes of the slice: x: 4, y: 4, z: 16, core: 2. Of those that a mesh axis runs over, the one named last changes fastest.
Arguments:
- face_grads: bfloat16 [32768, 2048], P('dp', 'tensor'), may hold values from -6 to 6
- face_owner: int32 [32768, 1], P('dp'), may hold values from 0 to 127; in each aligned block of 256 rows (0 to 255, 256 to 511, ...) at most 4 rows name the same one
- face_slot: int32 [32768, 1], P('dp'), may hold values from 0 to 255
- queries: bfloat16 [32768, 1024], P('dp', 'tensor'), may hold values from -6 to 6
- context_keys: bfloat16 [512, 1024], P(None, 'tensor'), may hold values from -6 to 6
- context_values: bfloat16 [512, 1024], P(None, 'tensor'), may hold values from -6 to 6
- w_out: bfloat16 [1024, 2048], P('tensor'), may hold values from -0.1875 to 0.1875
- branch_gate: float32 [2048], replicated, may hold values from 0.3 to 3
Outputs:
- grad_q: bfloat16 [32768, 1024], P('dp', 'tensor')
- grad_wo_t: float32 [2048, 1024], P('dp', 'tensor')
- grad_k: float32 [512, 1024], P('dp', 'tensor')
- grad_v: float32 [512, 1024], P('dp', 'tensor')
Inputs may be any that keep to these rules, and one draw needn't show every extreme that they name: `face_owner`: at most 4 of the 256 face rows of one dp index name the same owner.
All inputs are finite; a program needn't handle non-finite values.
Results may differ from a plain program's by a relative error of at most 0.03.
Values may be sent and summed in bfloat16 or wider, within the bound.
A program may use at most 64 MiB of HBM per device.

v0:
```python
import math

import jax
import jax.numpy as jnp
from jax import lax
from jax.sharding import PartitionSpec as P

HD = 128


def route_rows(face_block, face_owner, face_slot, num_dp, tok_rows):
    face_rows = face_block.shape[0]
    capacity = 2 * face_rows // num_dp
    owner_index = face_owner[:, 0]
    marker = (owner_index[:, None] == jnp.arange(num_dp, dtype=jnp.int32)[None, :]).astype(
        jnp.int32
    )
    earlier = jnp.cumsum(marker, axis=0) - marker
    in_bucket = jnp.sum(earlier * marker, axis=1)
    places = owner_index * capacity + in_bucket
    outgoing = (
        jnp.zeros((num_dp * capacity, face_block.shape[1]), face_block.dtype)
        .at[places]
        .set(face_block)
    )
    targets = jnp.full((num_dp * capacity,), tok_rows, jnp.int32).at[places].set(face_slot[:, 0])
    return (
        outgoing.reshape(num_dp, capacity, face_block.shape[1]),
        targets.reshape(num_dp, capacity),
    )


def land_rows(arrived, landed, tok_rows):
    row_width = arrived.shape[2]
    summed = jax.ops.segment_sum(
        arrived.reshape(-1, row_width).astype(jnp.float32),
        landed.reshape(-1),
        num_segments=tok_rows + 1,
    )
    return summed[:tok_rows].astype(jnp.bfloat16)


def body(
    face_grads, face_owner, face_slot, queries, context_keys, context_values, w_out, branch_gate
):
    num_dp = lax.axis_size("dp")
    tok_rows = queries.shape[0]
    full_faces = lax.all_gather(face_grads, "tensor", axis=1, tiled=True)
    outgoing, targets = route_rows(full_faces, face_owner, face_slot, num_dp, tok_rows)
    arrived, landed = (
        lax.all_to_all(outgoing, "dp", split_axis=0, concat_axis=0, tiled=True),
        lax.all_to_all(targets, "dp", split_axis=0, concat_axis=0, tiled=True),
    )
    grad_out = land_rows(arrived, landed, tok_rows)
    branch_grad = (branch_gate[None, :] * grad_out.astype(jnp.float32)).astype(jnp.bfloat16)
    grad_attn = lax.dot_general(
        branch_grad, w_out, (((1,), (1,)), ((), ())), preferred_element_type=jnp.float32
    ).astype(jnp.bfloat16)
    local_heads = queries.shape[1] // HD
    context_rows = context_keys.shape[0]
    score_scale = 1.0 / math.sqrt(HD)
    query_heads = queries.reshape(tok_rows, local_heads, HD)
    key_heads = context_keys.reshape(context_rows, local_heads, HD)
    value_heads = context_values.reshape(context_rows, local_heads, HD)
    attn_grad = grad_attn.reshape(tok_rows, local_heads, HD)
    scores = (
        jnp.einsum("thd,chd->htc", query_heads, key_heads, preferred_element_type=jnp.float32)
        * score_scale
    )
    weights = jax.nn.softmax(scores, axis=-1)
    probs = weights.astype(jnp.bfloat16)
    attention = (
        jnp.einsum("htc,chd->thd", probs, value_heads, preferred_element_type=jnp.float32)
        .astype(jnp.bfloat16)
        .reshape(tok_rows, local_heads * HD)
    )
    grad_probs = jnp.einsum(
        "thd,chd->htc", attn_grad, value_heads, preferred_element_type=jnp.float32
    )
    row_delta = jnp.sum(weights * grad_probs, axis=-1, keepdims=True)
    score_grad = (weights * (grad_probs - row_delta)).astype(jnp.bfloat16)
    grad_q = (
        (
            score_scale
            * jnp.einsum("htc,chd->thd", score_grad, key_heads, preferred_element_type=jnp.float32)
        )
        .astype(jnp.bfloat16)
        .reshape(tok_rows, local_heads * HD)
    )
    key_term = score_scale * jnp.einsum(
        "htc,thd->chd", score_grad, query_heads, preferred_element_type=jnp.float32
    )
    value_term = jnp.einsum("htc,thd->chd", probs, attn_grad, preferred_element_type=jnp.float32)
    grad_k, grad_v = (
        lax.psum_scatter(
            key_term.reshape(context_rows, local_heads * HD), "dp", scatter_dimension=0, tiled=True
        ),
        lax.psum_scatter(
            value_term.reshape(context_rows, local_heads * HD),
            "dp",
            scatter_dimension=0,
            tiled=True,
        ),
    )
    grad_wo_t = lax.psum_scatter(
        lax.dot_general(
            branch_grad, attention, (((0,), (0,)), ((), ())), preferred_element_type=jnp.float32
        ),
        "dp",
        scatter_dimension=0,
        tiled=True,
    )
    return (grad_q, grad_wo_t, grad_k, grad_v)


def solution(mesh):
    in_specs = (
        P("dp", "tensor"),
        P("dp", None),
        P("dp", None),
        P("dp", "tensor"),
        P(None, "tensor"),
        P(None, "tensor"),
        P("tensor", None),
        P(),
    )
    out_specs = (P("dp", "tensor"), P("dp", "tensor"), P("dp", "tensor"), P("dp", "tensor"))
    return jax.shard_map(body, mesh=mesh, in_specs=in_specs, out_specs=out_specs, check_vma=False)
```

profile of v0, /device:TPU:1, one launch (start us, length us, event | category | flops | bytes accessed | tf_op | source)
XLA Modules:
  0.0 779.8 jit_solution(146063908504578974)
XLA Ops:
  7.2 0.0 copy-start
  7.2 0.0 all-gather.2.cloned.1.call-start
  7.2 0.7 all-gather.2.cloned.1.call-update
  7.9 0.8 copy.37
  8.7 0.2 fusion.12
  9.0 0.9 fusion.14
  9.9 0.7 compare_select_fusion
  10.6 1.6 scatter_custom_fusion
  12.1 0.7 all_to_all.9
  12.9 20.6 %all-to-all-start = ((s32[128,1,4]{2,1,0:T(1,128)}), s32[128,1,4]{2,1,0:T(1,128)S(1)}, u32[]{:S(2)}, u32[]{:S(2)}) async-start(s32[128,1,4]{2,1,0:T(1,128)} %bitcast.8), calls=%async_computation | async-start | bytes 131072 | tf_op jit(solution)/shard_map/all_to_all | solution.py:52
  33.4 12.7 %all-gather.2.cloned.1.call-done = bf16[256,2048]{1,0:T(8,128)(2,1)} async-done(((bf16[256,512]{1,0:T(8,128)(2,1)}), bf16[256,2048]{1,0:T(8,128)(2,1)}) %all-gather.2.cloned.1.call-update) | async-done | bytes 1048592 | tf_op jit(solution)/shard_map/all_gather | solution.py:48
  46.2 3.5 scatter_custom_fusion.1
  49.7 2.2 reshape.67
  51.9 0.0 copy-start.7
  51.9 0.0 all-to-all-done
  51.9 0.0 copy-start.6
  51.9 0.6 copy-done.6
  52.5 17.6 %all-to-all-start.1 = ((bf16[128,4,2048]{2,1,0:T(4,128)(2,1)}), bf16[128,4,2048]{2,1,0:T(4,128)(2,1)S(1)}, u32[]{:S(2)}, u32[]{:S(2)}) async-start(bf16[128,4,2048]{2,1,0:T(4,128)(2,1)} %reshape.67), calls=%async_computation.1 | async-start | bytes 4194304 | tf_op jit(solution)/shard_map/all_to_all | solution.py:51
  70.1 0.2 all-reduce.5.cloned.1.call-start
  70.3 0.0 copy-done.7
  70.3 0.1 copy.49
  70.4 0.0 copy-start.4
  70.5 1.1 copy.50
  71.6 1.8 copy.51
  73.4 1.5 fusion.21
  74.9 0.5 broadcast.42
  75.4 2.3 reduce.3
  77.7 0.9 reshape.93
  78.6 90.6 %all-to-all-done.1 = bf16[128,4,2048]{2,1,0:T(4,128)(2,1)S(1)} async-done(((bf16[128,4,2048]{2,1,0:T(4,128)(2,1)}), bf16[128,4,2048]{2,1,0:T(4,128)(2,1)S(1)}, u32[]{:S(2)}, u32[]{:S(2)}) %all-to-all-start.1) | async-done | bytes 2097184 | tf_op jit(solution)/shard_map/all_to_all | solution.py:51
  169.2 0.0 copy-done.4
  169.2 2.5 reshape.95
  171.7 0.0 copy-start.8
  171.7 9.0 %scatter_custom_fusion.2 = f32[257,2048]{1,0:T(8,128)S(1)} fusion(s32[512]{0:T(512)S(1)} %reshape.93, f32[512,2048]{1,0:T(8,128)} %reshape.95, f32[]{:T(128)} %constant.10.clone.1), kind=kCustom, calls=%fused_computation.14 | custom fusion | flops 1048576 | bytes 2105856 | tf_op jit(solution)/shard_map/scatter-add | solution.py:35
  180.7 0.0 copy-done
  180.7 0.0 copy-done.8
  180.7 1.1 convolution_convert_fusion.1
  181.8 2.5 fusion.9
  184.3 0.0 copy-start.3
  184.3 1.9 multiply_reduce_fusion
  186.2 0.0 copy-start.5
  186.2 0.0 copy-done.3
  186.2 0.2 multiply_convert_fusion.1
  186.4 0.0 copy-start.1
  186.5 0.8 copy-done.1
  187.2 0.0 copy-done.5
  187.2 1.0 convolution_multiply_fusion.1
  188.3 2.1 copy.45
  190.3 2.0 copy.46
  192.4 0.0 all-reduce.5.cloned.1.call-update
  192.4 0.0 reduce-scatter.2.cloned.1.call-start
  192.4 2.4 convolution_convert_fusion
  194.9 2.8 fusion.8
  197.6 0.0 copy-start.2
  197.6 0.0 reduce-scatter.2.cloned.1.call-update
  197.7 1.3 dynamic-slice
  199.6 0.0 copy-done.2
  199.6 0.3 fusion.3
  199.9 0.8 copy.47
  200.7 318.8 %all-reduce.5.cloned.1.call-done = (f32[512,256]{1,0:T(8,128)}, f32[512,256]{1,0:T(8,128)}) async-done(((f32[512,256]{1,0:T(8,128)}, f32[512,256]{1,0:T(8,128)}), (f32[512,256]{1,0:T(8,128)}, f32[512,256]{1,0:T(8,128)})) %all-reduce.5.cloned.1.call-update) | async-done | bytes 1048592
  519.5 1.3 constant_dynamic-slice_fusion
  520.8 252.4 %reduce-scatter.2.cloned.1.call-done = f32[16,256]{1,0:T(8,128)} async-done(((f32[2048,256]{1,0:T(8,128)}), f32[16,256]{1,0:T(8,128)}) %reduce-scatter.2.cloned.1.call-update) | async-done | bytes 16400 | tf_op jit(solution)/shard_map/reduce_scatter | solution.py:105
  (6 shorter events, 0.1 us)
Async XLA Ops:
  7.2 173.5 %copy-start = (bf16[256,2048]{1,0:T(8,128)(2,1)S(1)}, bf16[256,2048]{1,0:T(8,128)(2,1)}, u32[]{:S(2)}) copy-start(bf16[256,2048]{1,0:T(8,128)(2,1)} %param.14) | copy-start | bytes 3145732
  7.2 39.0 %all-gather.2.cloned.1.call-start = ((), (), s32[]{:S(2)}) async-start(), calls=%async_computation.3 | async-start | bytes 1310720 | tf_op jit(solution)/shard_map/all_gather | solution.py:48
  12.9 39.1 %all-to-all-start = ((s32[128,1,4]{2,1,0:T(1,128)}), s32[128,1,4]{2,1,0:T(1,128)S(1)}, u32[]{:S(2)}, u32[]{:S(2)}) async-start(s32[128,1,4]{2,1,0:T(1,128)} %bitcast.8), calls=%async_computation | async-start | bytes 131072 | tf_op jit(solution)/shard_map/all_to_all | solution.py:52
  51.9 18.4 %copy-start.7 = (bf16[256,256]{1,0:T(8,128)(2,1)S(1)}, bf16[256,256]{1,0:T(8,128)(2,1)}, u32[]{:S(2)}) copy-start(bf16[256,256]{1,0:T(8,128)(2,1)} %param.11) | copy-start | bytes 393220
  51.9 0.6 copy-start.6
  52.5 116.7 %all-to-all-start.1 = ((bf16[128,4,2048]{2,1,0:T(4,128)(2,1)}), bf16[128,4,2048]{2,1,0:T(4,128)(2,1)S(1)}, u32[]{:S(2)}, u32[]{:S(2)}) async-start(bf16[128,4,2048]{2,1,0:T(4,128)(2,1)} %reshape.67), calls=%async_computation.1 | async-start | bytes 4194304 | tf_op jit(solution)/shard_map/all_to_all | solution.py:51
  70.1 449.4 %all-reduce.5.cloned.1.call-start = ((), (), s32[]{:S(2)}) async-start(), calls=%async_computation.5 | async-start | bytes 2097152
  70.4 98.8 %copy-start.4 = (bf16[256,256]{0,1:T(8,128)(2,1)}, bf16[256,256]{0,1:T(8,128)(2,1)S(1)}, u32[]{:S(2)}) copy-start(bf16[256,256]{0,1:T(8,128)(2,1)S(1)} %copy.49) | copy-start | bytes 393220
  171.7 9.0 %copy-start.8 = (f32[2048]{0:T(1024)S(1)}, f32[2048]{0:T(1024)}, u32[]{:S(2)}) copy-start(f32[2048]{0:T(1024)} %param.15) | copy-start | bytes 24580
  184.3 1.9 copy-start.3
  186.2 1.0 copy-start.5
  186.4 0.8 copy-start.1
  192.4 580.9 %reduce-scatter.2.cloned.1.call-start = ((), (), s32[]{:S(2)}) async-start(), calls=%async_computation.4 | async-start | bytes 2113536 | tf_op jit(solution)/shard_map/reduce_scatter | solution.py:105
  197.6 2.0 copy-start.2
Sparse Core Ops, SparseCore 0:
  10.1 36.0 all-gather.1
  192.5 326.9 all-reduce.4
  525.4 247.8 reduce-scatter.1
where the time goes:
time: 791 us; the launch traced here: 780 us
  waiting for transfers between devices  675 us (85%)
  starting transfers between devices  38.4 us (5%)
  local copies, waits for them, and re-layouts  24.7 us (3%)
  between operations  14.6 us (2%)
  matrix products  13.5 us (2%)
  other arithmetic  13.3 us (2%)
    unnamed x4, waiting for transfers between devices  320 us
    reduce_scatter x1, waiting for transfers between devices, body(): lax.psum_scatter(lax.dot_general(branch_grad, attention, (((0,), (0,)), (...  252 us
    all_to_all x1, waiting for transfers between devices, body(): lax.all_to_all(outgoing, 'dp', split_axis=0, concat_axis=0, tiled=True)  90.6 us
    all_to_all x1, starting transfers between devices, body(): lax.all_to_all(targets, 'dp', split_axis=0, concat_axis=0, tiled=True)  20.6 us
    all_to_all x1, starting transfers between devices, body(): lax.all_to_all(outgoing, 'dp', split_axis=0, concat_axis=0, tiled=True)  17.6 us
  transfers between devices with their start and end apart: 5, of which 4 were waited for; matrix products, arithmetic and copies ran while one was open for 3% of the time, Pallas kernels for 0%

commit v1 on v0

v1 whole, which is shorter than its diff:
```python
import functools
import math

import jax
import jax.numpy as jnp
from jax import lax
from jax.experimental import pallas as pl
from jax.experimental.pallas import tpu as pltpu
from jax.sharding import PartitionSpec as P

HD = 128
LANES = 128
CORES = 2
MESH = pl.DeviceIdType.MESH
F32 = jnp.float32
BF16 = jnp.bfloat16


def iota(shape, axis):
    return lax.broadcasted_iota(jnp.int32, shape, axis)


def log2(n):
    bits = n.bit_length() - 1
    assert 1 << bits == n
    return bits


def one_hot(cond):
    return jnp.where(cond, 1.0, 0.0).astype(BF16)


def dot(a, b, dims=((1,), (0,))):
    return lax.dot_general(a, b, (dims, ((), ())), preferred_element_type=F32)


NT = ((1,), (1,))
TN = ((0,), (0,))


def kernel(
    nx,
    nz,
    face_ref,
    owner_ref,
    slot_ref,
    q_ref,
    k_ref,
    v_ref,
    w_ref,
    gate_ref,
    gq_ref,
    gwo_ref,
    gk_ref,
    gv_ref,
    out_a,
    in_a,
    mout_a,
    min_a,
    m2d,
    min_b,
    out_b,
    in_b,
    wall,
    aall,
    ga_out,
    ga_in,
    wo_out,
    wo_in,
    wz_out,
    wz_in,
    kv_out,
    kv_in,
    kz_out,
    kz_in,
    wts,
    probs,
    kp,
    vp,
    bg,
    perm_b,
    send,
    recv_a,
    recv_b,
    recv,
):
    ny = nx
    np_ = ny * CORES
    ch, _, ma, _ = out_a.shape
    faces, dx = face_ref.shape
    tok, hw = q_ref.shape
    ctx = k_ref.shape[0]
    heads = hw // HD
    places = nz * ma
    cap = ma // np_
    rw = gwo_ref.shape[0]
    kr = gk_ref.shape[0]
    halves = hw // LANES
    lanes_m = m2d.shape[1]
    scale = 1.0 / math.sqrt(HD)

    d = lax.axis_index("dp")
    x = lax.axis_index("tensor")
    c = lax.rem(d, CORES)
    z = lax.rem(lax.div(d, CORES), nz)
    y = lax.div(d, CORES * nz)
    p = y * CORES + c

    def z_peer(k):
        zz = lax.rem(z + k, nz)
        return zz, (y * nz + zz) * CORES + c

    def p_peer(k):
        pp = lax.rem(p + k, np_)
        return pp, (lax.div(pp, CORES) * nz + z) * CORES + lax.rem(pp, CORES)

    def t_peer(k):
        zz = lax.rem(z + k, nz)
        return zz, (x * nz + zz) * CORES + c

    def loop(lo, hi, f):
        def step(i, carry):
            f(i)
            return carry

        lax.fori_loop(lo, hi, step, 0)

    def push(src, dst, ssem, rsem, dev):
        pltpu.make_async_remote_copy(
            src_ref=src, dst_ref=dst, send_sem=ssem, recv_sem=rsem, device_id=dev, device_id_type=MESH
        ).start()

    def wait_recv(view, rsem):
        pltpu.make_async_remote_copy(
            src_ref=view, dst_ref=view, send_sem=send.at[0], recv_sem=rsem, device_id=(d, x), device_id_type=MESH
        ).wait_recv()

    def wait_send(view, ssem):
        pltpu.make_async_remote_copy(
            src_ref=view, dst_ref=view, send_sem=ssem, recv_sem=recv.at[0], device_id=(d, x), device_id_type=MESH
        ).wait_send()

    barrier = pltpu.get_barrier_semaphore()

    def greet(dev):
        pl.semaphore_signal(barrier, inc=1, device_id=dev, device_id_type=MESH)

    loop(1, nz, lambda k: greet((z_peer(k)[1], x)))
    loop(1, np_, lambda k: greet((p_peer(k)[1], x)))
    loop(1, nx, lambda k: greet((d, lax.rem(x + k, nx))))

    @pl.when(x != y)
    def _():
        loop(0, nz, lambda k: greet((t_peer(k)[1], y)))

    owner = owner_ref[...]
    owner_f = owner.astype(F32)
    sub, lane = iota((faces, faces), 0), iota((faces, faces), 1)
    owner_col = jnp.sum(jnp.where(sub == lane, owner_f, 0.0), axis=1, keepdims=True)
    rank = jnp.sum(
        jnp.where((owner_col == owner_f) & (sub < lane), 1.0, 0.0), axis=0, keepdims=True
    ).astype(jnp.int32)
    oc = owner & (CORES - 1)
    oz = (owner >> log2(CORES)) & (nz - 1)
    oy = owner >> log2(CORES * nz)
    place = ((oz * ny + oy) * CORES + oc) * cap + rank
    placed = iota((places, faces), 0) == place
    slot_col = (
        jnp.sum(jnp.where(placed, slot_ref[...].astype(F32) + 1.0, 0.0), axis=1, keepdims=True) - 1.0
    )
    spread = jnp.where(
        iota((places, lanes_m), 1) == (iota((places, lanes_m), 0) & (ma - 1)), slot_col, 0.0
    ).astype(BF16)
    by_z = one_hot(iota((nz, places), 0) == (iota((nz, places), 1) >> log2(ma)))
    meta = dot(by_z, spread)
    for i in range(nz):
        mout_a[i] = meta[i : i + 1, :]
    min_a[z] = mout_a[z]
    place_hot = one_hot(placed)

    def fill(i):
        part = dot(place_hot, face_ref[:, i * LANES : (i + 1) * LANES]).astype(BF16)
        out_a[i] = part.reshape(nz, ma, LANES)
        in_a[i, z] = out_a[i, z]

    fill(0)
    pl.semaphore_wait(barrier, (nz - 1) + (np_ - 1) + (nx - 1) + jnp.where(x == y, 0, nz))

    def send_meta(k):
        zz, dev = z_peer(k)
        push(mout_a.at[zz], min_a.at[z], send.at[0], recv.at[0], (dev, x))

    loop(1, nz, send_meta)

    def send_a(i):
        def step(k):
            zz, dev = z_peer(k)
            push(out_a.at[i, zz], in_a.at[i, z], send.at[1], recv_a.at[i], (dev, x))

        loop(1, nz, step)

    send_a(0)

    def send_w(k):
        xx = lax.rem(x + k, nx)
        push(
            w_ref.at[:, pl.ds(pl.multiple_of(xx * dx, LANES), dx)],
            wall.at[x],
            send.at[2],
            recv.at[1],
            (d, xx),
        )

    loop(1, nx, send_w)
    for i in range(1, ch):
        fill(i)
        send_a(i)
    wall[x] = w_ref[:, pl.ds(pl.multiple_of(x * dx, LANES), dx)]

    new, old = iota((ctx, ctx), 0), iota((ctx, ctx), 1)
    b_k, b_z, b_c = log2(kr), log2(nz), log2(CORES)
    o_k = old & (kr - 1)
    o_c = (old >> b_k) & (CORES - 1)
    o_z = (old >> (b_k + b_c)) & (nz - 1)
    o_y = old >> (b_k + b_c + b_z)
    perm_k = one_hot(new == ((o_y * CORES + o_c) * nz + o_z) * kr + o_k)
    kp[...] = dot(perm_k, k_ref[...]).astype(BF16)
    vp[...] = dot(perm_k, v_ref[...]).astype(BF16)
    for h in range(heads):
        cols = slice(h * HD, (h + 1) * HD)
        scores = dot(q_ref[:, cols], kp[:, cols], NT) * scale
        top = jnp.max(scores, axis=-1, keepdims=True)
        e = jnp.exp(scores - top)
        w = e / jnp.sum(e, axis=-1, keepdims=True)
        wts[h] = w
        pb = w.astype(BF16)
        probs[h] = pb
        aall[x, :, cols] = dot(pb, vp[:, cols]).astype(BF16)

    def send_att(k):
        xx = lax.rem(x + k, nx)
        push(aall.at[x], aall.at[x], send.at[3], recv.at[2], (d, xx))

    loop(1, nx, send_att)

    new, old = iota((places, places), 0), iota((places, places), 1)
    o_r = old & (cap - 1)
    o_p = (old >> log2(cap)) & (np_ - 1)
    o_z = old >> log2(ma)
    perm_b[...] = one_hot(new == (o_p * nz + o_z) * cap + o_r)

    wait_recv(min_a.at[pl.ds(0, nz - 1)], recv.at[0])
    for i in range(nz):
        m2d[i : i + 1, :] = min_a[i]
    min_b[p] = m2d[...]

    def send_mb(k):
        _, dev = p_peer(k)
        push(m2d, min_b.at[p], send.at[4], recv.at[3], (dev, x))

    loop(1, np_, send_mb)

    for i in range(ch):
        wait_recv(in_a.at[i, pl.ds(0, nz - 1)], recv_a.at[i])
        moved = dot(perm_b[...], in_a[i].reshape(places, LANES)).astype(BF16)
        out_b[i] = moved.reshape(np_, nz * cap, LANES)
        in_b[i, p] = out_b[i, p]

        def send_b(k, i=i):
            pp, dev = p_peer(k)
            push(out_b.at[i, pp], in_b.at[i, p], send.at[5], recv_b.at[i], (dev, x))

        loop(1, np_, send_b)

    wait_recv(min_b.at[pl.ds(0, np_ - 1)], recv.at[3])
    pick = one_hot(
        iota((lanes_m, places), 0) == p * cap + (iota((lanes_m, places), 1) & (cap - 1))
    )
    table = dot(min_b[...].reshape(np_ * nz, lanes_m).astype(BF16), pick)
    slot_row = jnp.sum(
        jnp.where(
            iota((np_ * nz, places), 0) == (iota((np_ * nz, places), 1) >> log2(cap)), table, 0.0
        ),
        axis=0,
        keepdims=True,
    )
    land = one_hot(iota((tok, places), 0).astype(F32) == slot_row)
    gate = gate_ref[:, pl.ds(pl.multiple_of(x * dx, LANES), dx)]
    for i in range(ch):
        cols = slice(i * LANES, (i + 1) * LANES)
        wait_recv(in_b.at[i, pl.ds(0, np_ - 1)], recv_b.at[i])
        grad_out = dot(land, in_b[i].reshape(places, LANES)).astype(BF16)
        bg[:, cols] = (gate[:, cols] * grad_out.astype(F32)).astype(BF16)

    wait_recv(wall.at[pl.ds(0, nx - 1)], recv.at[1])

    def project(k):
        xx = lax.rem(x + k, nx)
        ga_out[xx] = dot(bg[...], wall[xx], NT).astype(BF16)
        push(ga_out.at[xx], ga_in.at[x], send.at[6], recv.at[4], (d, xx))

    loop(1, nx, project)
    ga_in[x] = dot(bg[...], wall[x], NT).astype(BF16)

    wait_recv(aall.at[pl.ds(0, nx - 1)], recv.at[2])

    def outer(xx):
        part = dot(bg[...], aall[xx], TN).astype(BF16).reshape(nz, CORES, rw, hw)
        for cc in range(CORES):
            wo_out[xx * CORES + cc] = part[:, cc]

    loop(0, ny, outer)
    wo_in[p] = wo_out[p]

    def send_wo(k):
        pp, dev = p_peer(k)
        push(wo_out.at[pp], wo_in.at[p], send.at[7], recv.at[5], (dev, x))

    loop(1, np_, send_wo)

    wait_recv(ga_in.at[pl.ds(0, nx - 1)], recv.at[4])
    total = ga_in[0].astype(F32)
    for i in range(1, nx):
        total = total + ga_in[i].astype(F32)
    ga = total.astype(BF16)
    for h in range(heads):
        cols = slice(h * HD, (h + 1) * HD)
        ga_h = ga[:, cols]
        gp = dot(ga_h, vp[:, cols], NT)
        w = wts[h]
        delta = jnp.sum(w * gp, axis=-1, keepdims=True)
        sg = (w * (gp - delta)).astype(BF16)
        gk_h = (scale * dot(sg, q_ref[:, cols], TN)).astype(BF16)
        gv_h = dot(probs[h], ga_h, TN).astype(BF16)
        kv_out[:, 0, :, cols] = gk_h.reshape(np_, nz * kr, HD)
        kv_out[:, 1, :, cols] = gv_h.reshape(np_, nz * kr, HD)
        gq_ref[:, cols] = (scale * dot(sg, kp[:, cols])).astype(BF16)
    kv_in[p] = kv_out[p]

    def send_kv(k):
        pp, dev = p_peer(k)
        push(kv_out.at[pp], kv_in.at[p], send.at[8], recv.at[6], (dev, x))

    loop(1, np_, send_kv)

    wait_recv(wo_in.at[pl.ds(0, np_ - 1)], recv.at[5])

    def sum_wo(i):
        acc = wo_in[0, i].astype(F32)
        for j in range(1, np_):
            acc = acc + wo_in[j, i].astype(F32)
        wz_out[i] = acc.astype(BF16)

    loop(0, nz, sum_wo)

    def send_wz(k):
        zz, dev = t_peer(k)
        push(wz_out.at[zz], wz_in.at[z], send.at[9], recv.at[7], (dev, y))

    @pl.when(x != y)
    def _():
        send_wz(0)

    @pl.when(x == y)
    def _():
        wz_in[z] = wz_out[z]

    loop(1, nz, send_wz)

    wait_recv(kv_in.at[pl.ds(0, np_ - 1)], recv.at[6])
    rows = 2 * halves * kr
    acc = None
    for j in range(2):
        tot = kv_in[0, j].astype(F32)
        for i in range(1, np_):
            tot = tot + kv_in[i, j].astype(F32)
        tot = tot.astype(BF16)
        for h in range(halves):
            r, s = iota((nz * rows, nz * kr), 0), iota((nz * rows, nz * kr), 1)
            inner = r & (rows - 1)
            sel = (
                ((r >> log2(rows)) == (s >> b_k))
                & ((inner >> b_k) == j * halves + h)
                & ((inner & (kr - 1)) == (s & (kr - 1)))
            )
            part = dot(one_hot(sel), tot[:, h * LANES : (h + 1) * LANES])
            acc = part if acc is None else acc + part
    kz_out[...] = acc.astype(BF16).reshape(nz, rows, LANES)
    kz_in[z] = kz_out[z]

    def send_kz(k):
        zz, dev = z_peer(k)
        push(kz_out.at[zz], kz_in.at[z], send.at[10], recv.at[8], (dev, x))

    loop(1, nz, send_kz)

    @pl.when(x != y)
    def _():
        wait_recv(wz_in, recv.at[7])

    @pl.when(x == y)
    def _():
        wait_recv(wz_in.at[pl.ds(0, nz - 1)], recv.at[7])

    acc = wz_in[0].astype(F32)
    for i in range(1, nz):
        acc = acc + wz_in[i].astype(F32)
    gwo_ref[...] = acc

    wait_recv(kz_in.at[pl.ds(0, nz - 1)], recv.at[8])
    acc = kz_in[0].astype(F32)
    for i in range(1, nz):
        acc = acc + kz_in[i].astype(F32)
    for h in range(halves):
        cols = slice(h * LANES, (h + 1) * LANES)
        gk_ref[:, cols] = acc[h * kr : (h + 1) * kr, :]
        gv_ref[:, cols] = acc[(halves + h) * kr : (halves + h + 1) * kr, :]

    wait_send(mout_a.at[pl.ds(0, nz - 1)], send.at[0])
    wait_send(out_a.at[:, pl.ds(0, nz - 1)], send.at[1])
    wait_send(wall.at[pl.ds(0, nx - 1)], send.at[2])
    wait_send(aall.at[pl.ds(0, nx - 1)], send.at[3])
    wait_send(min_b.at[pl.ds(0, np_ - 1)], send.at[4])
    wait_send(out_b.at[:, pl.ds(0, np_ - 1)], send.at[5])
    wait_send(ga_out.at[pl.ds(0, nx - 1)], send.at[6])
    wait_send(wo_out.at[pl.ds(0, np_ - 1)], send.at[7])
    wait_send(kv_out.at[pl.ds(0, np_ - 1)], send.at[8])

    @pl.when(x != y)
    def _():
        wait_send(wz_out, send.at[9])

    @pl.when(x == y)
    def _():
        wait_send(wz_out.at[pl.ds(0, nz - 1)], send.at[9])

    wait_send(kz_out.at[pl.ds(0, nz - 1)], send.at[10])


def body(face_grads, face_owner, face_slot, queries, keys, values, w_out, branch_gate):
    nx = lax.axis_size("tensor")
    dp = lax.axis_size("dp")
    ny = nx
    nz = dp // (ny * CORES)
    np_ = ny * CORES
    faces, dx = face_grads.shape
    tok, hw = queries.shape
    ctx = keys.shape[0]
    heads = hw // HD
    cap = 2 * faces // dp
    ch = dx // LANES
    ma = np_ * cap
    places = nz * ma
    width = w_out.shape[1]
    rw = width // dp
    kr = ctx // dp
    rows = 2 * (hw // LANES) * kr
    lanes_m = max(LANES, ma)
    vmem = pltpu.VMEM
    dma = pltpu.SemaphoreType.DMA
    spec = pl.BlockSpec(memory_space=pltpu.VMEM)
    return pl.pallas_call(
        functools.partial(kernel, nx, nz),
        out_shape=(
            jax.ShapeDtypeStruct((tok, hw), BF16),
            jax.ShapeDtypeStruct((rw, hw), F32),
            jax.ShapeDtypeStruct((kr, hw), F32),
            jax.ShapeDtypeStruct((kr, hw), F32),
        ),
        in_specs=[spec] * 8,
        out_specs=(spec,) * 4,
        scratch_shapes=[
            vmem((ch, nz, ma, LANES), BF16),
            vmem((ch, nz, ma, LANES), BF16),
            vmem((nz, 1, lanes_m), F32),
            vmem((nz, 1, lanes_m), F32),
            vmem((nz, lanes_m), F32),
            vmem((np_, nz, lanes_m), F32),
            vmem((ch, np_, nz * cap, LANES), BF16),
            vmem((ch, np_, nz * cap, LANES), BF16),
            vmem((nx, hw, dx), BF16),
            vmem((nx, tok, hw), BF16),
            vmem((nx, tok, hw), BF16),
            vmem((nx, tok, hw), BF16),
            vmem((np_, nz, rw, hw), BF16),
            vmem((np_, nz, rw, hw), BF16),
            vmem((nz, rw, hw), BF16),
            vmem((nz, rw, hw), BF16),
            vmem((np_, 2, nz * kr, hw), BF16),
            vmem((np_, 2, nz * kr, hw), BF16),
            vmem((nz, rows, LANES), BF16),
            vmem((nz, rows, LANES), BF16),
            vmem((heads, tok, ctx), F32),
            vmem((heads, tok, ctx), BF16),
            vmem((ctx, hw), BF16),
            vmem((ctx, hw), BF16),
            vmem((tok, dx), BF16),
            vmem((places, places), BF16),
            dma((11,)),
            dma((ch,)),
            dma((ch,)),
            dma((9,)),
        ],
        compiler_params=pltpu.CompilerParams(
            collective_id=0, has_side_effects=True, vmem_limit_bytes=44 << 20
        ),
    )(
        face_grads,
        face_owner.reshape(1, faces),
        face_slot.reshape(1, faces),
        queries,
        keys,
        values,
        w_out,
        branch_gate.reshape(1, width),
    )


def solution(mesh):
    in_specs = (
        P("dp", "tensor"),
        P("dp", None),
        P("dp", None),
        P("dp", "tensor"),
        P(None, "tensor"),
        P(None, "tensor"),
        P("tensor", None),
        P(),
    )
    out_specs = (P("dp", "tensor"), P("dp", "tensor"), P("dp", "tensor"), P("dp", "tensor"))
    return jax.shard_map(body, mesh=mesh, in_specs=in_specs, out_specs=out_specs, check_vma=False)
```

time: 791 us -> 96.5 us (0.12)
  the two profiles are of different devices: /device:TPU:1 before, /device:TPU:5 now
where the time goes in v1:
time: 96.5 us; the launch traced here: 96.2 us
  Pallas kernels  86.7 us (90%)
  local copies, waits for them, and re-layouts  8.8 us (9%)
    pallas_call x1, Pallas kernels, body(): pl.pallas_call(functools.partial(kernel, nx, nz), out_shape=(jax.ShapeDty...  86.7 us
    unnamed x20, local copies, waits for them, and re-layouts  8.8 us

profile of v1, /device:TPU:5, one launch (start us, length us, event | category | flops | bytes accessed | tf_op | source)
XLA Modules:
  0.0 96.2 jit_solution(5409399906737866705)
XLA Ops:
  0.6 0.0 copy-start.7
  0.6 0.0 copy-start.6
  0.7 0.7 copy-done.7
  1.3 0.0 copy-done.6
  1.3 0.0 copy-start
  1.3 1.2 %copy-done = bf16[256,2048]{1,0:T(8,128)(2,1)S(1)} copy-done((bf16[256,2048]{1,0:T(8,128)(2,1)S(1)}, bf16[256,2048]{1,0:T(8,128)(2,1)}, u32[]{:S(2)}) %copy-start) | copy-done | bytes 1048600
  2.6 0.0 copy-start.1
  2.6 0.9 copy-done.1
  3.5 0.0 copy-start.2
  3.5 0.9 copy-done.2
  4.5 0.0 copy-start.3
  4.5 0.9 copy-done.3
  5.4 0.0 copy-start.4
  5.4 0.9 copy-done.4
  6.3 0.0 copy-start.5
  6.3 0.7 copy-done.5
  7.0 86.7 %shard_map.111 = (bf16[256,256]{1,0:T(8,128)(2,1)S(1)}, f32[16,256]{1,0:T(8,128)S(1)}, f32[4,256]{1,0:T(4,128)S(1)}, f32[4,256]{1,0:T(4,128)S(1)}) custom-call(bf16[256,512]{1,0:T(8,128)(2,1)S(1)} %copy-done.1, s32[1,256]{1,0:T(1,128)S(1)} %bitcast.4, s32[1,256]{1,0:T(1,128)S(1)} %bitcast.5, bf16[256,256]{1,0:T(8,128)(2,1)S(1)} %copy-done.4, ...), custom_call_target="tpu_custom_call" | custom-call | tf_op jit(solution)/shard_map/pallas_call | solution.py:462
  93.8 0.7 copy.16
  94.4 0.6 copy.17
  95.0 0.6 copy.18
  95.6 0.6 copy.19
Async XLA Ops:
  0.6 0.7 copy-start.7
  0.6 0.7 copy-start.6
  1.3 1.2 %copy-start = (bf16[256,2048]{1,0:T(8,128)(2,1)S(1)}, bf16[256,2048]{1,0:T(8,128)(2,1)}, u32[]{:S(2)}) copy-start(bf16[256,2048]{1,0:T(8,128)(2,1)} %w_ref.1) | copy-start | bytes 3145732
  2.6 0.9 copy-start.1
  3.5 0.9 copy-start.2
  4.5 0.9 copy-start.3
  5.4 0.9 copy-start.4
  6.3 0.7 copy-start.5

commit v2 on v1

--- a/solution.py
+++ b/solution.py
@@ -41,14 +41,14 @@
 def kernel(
     nx,
     nz,
-    face_ref,
-    owner_ref,
-    slot_ref,
-    q_ref,
-    k_ref,
-    v_ref,
-    w_ref,
-    gate_ref,
+    face_hbm,
+    owner_hbm,
+    slot_hbm,
+    q_hbm,
+    k_hbm,
+    v_hbm,
+    w_hbm,
+    gate_hbm,
     gq_ref,
     gwo_ref,
     gk_ref,
@@ -61,29 +61,61 @@
     min_b,
     out_b,
     in_b,
-    wall,
     aall,
-    ga_out,
-    ga_in,
+    asib,
+    bgx,
+    bgt,
+    bgt_in,
     wo_out,
     wo_in,
     wz_out,
     wz_in,
-    kv_out,
-    kv_in,
+    kc_out,
+    kc_in,
+    ky_out,
+    ky_in,
     kz_out,
     kz_in,
     wts,
     probs,
     kp,
     vp,
-    bg,
+    ga_acc,
     perm_b,
+    perm_w,
+    w_ref,
+    face_ref,
+    owner_ref,
+    slot_ref,
+    q_ref,
+    k_ref,
+    v_ref,
+    gate_ref,
+    load,
     send,
     recv_a,
     recv_b,
+    recv_x,
     recv,
 ):
+    loads = [
+        pltpu.make_async_copy(src, dst, load.at[i])
+        for i, (src, dst) in enumerate(
+            (
+                (owner_hbm, owner_ref),
+                (slot_hbm, slot_ref),
+                (face_hbm, face_ref),
+                (k_hbm, k_ref),
+                (v_hbm, v_ref),
+                (q_hbm, q_ref),
+                (gate_hbm, gate_ref),
+                (w_hbm, w_ref),
+            )
+        )
+    ]
+    for copy in loads:
+        copy.start()
+
     ny = nx
     np_ = ny * CORES
     ch, _, ma, _ = out_a.shape
@@ -105,6 +137,7 @@
     z = lax.rem(lax.div(d, CORES), nz)
     y = lax.div(d, CORES * nz)
     p = y * CORES + c
+    twin = d + 1 - 2 * c
 
     def z_peer(k):
         zz = lax.rem(z + k, nz)
@@ -113,6 +146,10 @@
     def p_peer(k):
         pp = lax.rem(p + k, np_)
         return pp, (lax.div(pp, CORES) * nz + z) * CORES + lax.rem(pp, CORES)
+
+    def y_peer(k):
+        yy = lax.rem(y + k, ny)
+        return yy, (yy * nz + z) * CORES + c
 
     def t_peer(k):
         zz = lax.rem(z + k, nz)
@@ -153,6 +190,8 @@
     def _():
         loop(0, nz, lambda k: greet((t_peer(k)[1], y)))
 
+    loads[0].wait()
+    loads[1].wait()
     owner = owner_ref[...]
     owner_f = owner.astype(F32)
     sub, lane = iota((faces, faces), 0), iota((faces, faces), 1)
@@ -183,6 +222,7 @@
         out_a[i] = part.reshape(nz, ma, LANES)
         in_a[i, z] = out_a[i, z]
 
+    loads[2].wait()
     fill(0)
     pl.semaphore_wait(barrier, (nz - 1) + (np_ - 1) + (nx - 1) + jnp.where(x == y, 0, nz))
 
@@ -201,21 +241,11 @@
 
     send_a(0)
 
-    def send_w(k):
-        xx = lax.rem(x + k, nx)
-        push(
-            w_ref.at[:, pl.ds(pl.multiple_of(xx * dx, LANES), dx)],
-            wall.at[x],
-            send.at[2],
-            recv.at[1],
-            (d, xx),
-        )
-
-    loop(1, nx, send_w)
     for i in range(1, ch):
         fill(i)
         send_a(i)
-    wall[x] = w_ref[:, pl.ds(pl.multiple_of(x * dx, LANES), dx)]
+    for copy in loads[3:]:
+        copy.wait()
 
     new, old = iota((ctx, ctx), 0), iota((ctx, ctx), 1)
     b_k, b_z, b_c = log2(kr), log2(nz), log2(CORES)
@@ -223,7 +253,7 @@
     o_c = (old >> b_k) & (CORES - 1)
     o_z = (old >> (b_k + b_c)) & (nz - 1)
     o_y = old >> (b_k + b_c + b_z)
-    perm_k = one_hot(new == ((o_y * CORES + o_c) * nz + o_z) * kr + o_k)
+    perm_k = one_hot(new == ((o_c * ny + o_y) * nz + o_z) * kr + o_k)
     kp[...] = dot(perm_k, k_ref[...]).astype(BF16)
     vp[...] = dot(perm_k, v_ref[...]).astype(BF16)
     for h in range(heads):
@@ -248,6 +278,12 @@
     o_p = (old >> log2(cap)) & (np_ - 1)
     o_z = old >> log2(ma)
     perm_b[...] = one_hot(new == (o_p * nz + o_z) * cap + o_r)
+    new, old = iota((dx, dx), 0), iota((dx, dx), 1)
+    b_r = log2(rw)
+    o_r = old & (rw - 1)
+    o_c = (old >> b_r) & (CORES - 1)
+    o_z = old >> (b_r + b_c)
+    perm_w[...] = one_hot(new == (o_c * nz + o_z) * rw + o_r)
 
     wait_recv(min_a.at[pl.ds(0, nz - 1)], recv.at[0])
     for i in range(nz):
@@ -260,17 +296,19 @@
 
     loop(1, np_, send_mb)
 
-    for i in range(ch):
+    def forward(i):
         wait_recv(in_a.at[i, pl.ds(0, nz - 1)], recv_a.at[i])
         moved = dot(perm_b[...], in_a[i].reshape(places, LANES)).astype(BF16)
         out_b[i] = moved.reshape(np_, nz * cap, LANES)
         in_b[i, p] = out_b[i, p]
 
-        def send_b(k, i=i):
+        def step(k):
             pp, dev = p_peer(k)
             push(out_b.at[i, pp], in_b.at[i, p], send.at[5], recv_b.at[i], (dev, x))
 
-        loop(1, np_, send_b)
+        loop(1, np_, step)
+
+    forward(0)
 
     wait_recv(min_b.at[pl.ds(0, np_ - 1)], recv.at[3])
     pick = one_hot(
@@ -286,43 +324,64 @@
     )
     land = one_hot(iota((tok, places), 0).astype(F32) == slot_row)
     gate = gate_ref[:, pl.ds(pl.multiple_of(x * dx, LANES), dx)]
-    for i in range(ch):
-        cols = slice(i * LANES, (i + 1) * LANES)
+
+    def landing(i):
         wait_recv(in_b.at[i, pl.ds(0, np_ - 1)], recv_b.at[i])
         grad_out = dot(land, in_b[i].reshape(places, LANES)).astype(BF16)
-        bg[:, cols] = (gate[:, cols] * grad_out.astype(F32)).astype(BF16)
-
-    wait_recv(wall.at[pl.ds(0, nx - 1)], recv.at[1])
-
-    def project(k):
-        xx = lax.rem(x + k, nx)
-        ga_out[xx] = dot(bg[...], wall[xx], NT).astype(BF16)
-        push(ga_out.at[xx], ga_in.at[x], send.at[6], recv.at[4], (d, xx))
-
-    loop(1, nx, project)
-    ga_in[x] = dot(bg[...], wall[x], NT).astype(BF16)
+        bgx[i, x] = (gate[:, i * LANES : (i + 1) * LANES] * grad_out.astype(F32)).astype(BF16)
+
+        def step(k):
+            xx = lax.rem(x + k, nx)
+            push(bgx.at[i, x], bgx.at[i, x], send.at[6], recv_x.at[i], (d, xx))
+
+        loop(1, nx, step)
+
+    def project(i):
+        wait_recv(bgx.at[i, pl.ds(0, nx - 1)], recv_x.at[i])
+        part = None
+        for xx in range(nx):
+            first = xx * dx + i * LANES
+            term = dot(bgx[i, xx], w_ref[:, first : first + LANES], NT)
+            part = term if part is None else part + term
+        if i == 0:
+            ga_acc[...] = part
+        else:
+            ga_acc[...] += part
+
+    landing(0)
 
     wait_recv(aall.at[pl.ds(0, nx - 1)], recv.at[2])
+    push(aall, asib, send.at[2], recv.at[1], (twin, x))
+
+    for i in range(1, ch):
+        forward(i)
+        project(i - 1)
+        landing(i)
+
+    turned = None
+    for i in range(ch):
+        term = dot(perm_w[:, i * LANES : (i + 1) * LANES], bgx[i, x], NT)
+        turned = term if turned is None else turned + term
+    bgt[...] = turned.astype(BF16).reshape(CORES, nz * rw, tok)
+    push(bgt.at[1 - c], bgt_in, send.at[7], recv.at[4], (twin, x))
+    wait_recv(asib, recv.at[1])
+    wait_recv(bgt_in, recv.at[4])
 
     def outer(xx):
-        part = dot(bg[...], aall[xx], TN).astype(BF16).reshape(nz, CORES, rw, hw)
-        for cc in range(CORES):
-            wo_out[xx * CORES + cc] = part[:, cc]
+        part = dot(bgt[c], aall[xx]) + dot(bgt_in[...], asib[xx])
+        wo_out[xx] = part.astype(BF16).reshape(nz, rw, hw)
 
     loop(0, ny, outer)
-    wo_in[p] = wo_out[p]
+    wo_in[y] = wo_out[y]
 
     def send_wo(k):
-        pp, dev = p_peer(k)
-        push(wo_out.at[pp], wo_in.at[p], send.at[7], recv.at[5], (dev, x))
-
-    loop(1, np_, send_wo)
-
-    wait_recv(ga_in.at[pl.ds(0, nx - 1)], recv.at[4])
-    total = ga_in[0].astype(F32)
-    for i in range(1, nx):
-        total = total + ga_in[i].astype(F32)
-    ga = total.astype(BF16)
+        yy, dev = y_peer(k)
+        push(wo_out.at[yy], wo_in.at[y], send.at[8], recv.at[5], (dev, x))
+
+    loop(1, ny, send_wo)
+
+    project(ch - 1)
+    ga = ga_acc[...].astype(BF16)
     for h in range(heads):
         cols = slice(h * HD, (h + 1) * HD)
         ga_h = ga[:, cols]
@@ -332,22 +391,31 @@
         sg = (w * (gp - delta)).astype(BF16)
         gk_h = (scale * dot(sg, q_ref[:, cols], TN)).astype(BF16)
         gv_h = dot(probs[h], ga_h, TN).astype(BF16)
-        kv_out[:, 0, :, cols] = gk_h.reshape(np_, nz * kr, HD)
-        kv_out[:, 1, :, cols] = gv_h.reshape(np_, nz * kr, HD)
+        kc_out[:, 0, :, :, cols] = gk_h.reshape(CORES, ny, nz * kr, HD)
+        kc_out[:, 1, :, :, cols] = gv_h.reshape(CORES, ny, nz * kr, HD)
         gq_ref[:, cols] = (scale * dot(sg, kp[:, cols])).astype(BF16)
-    kv_in[p] = kv_out[p]
-
-    def send_kv(k):
-        pp, dev = p_peer(k)
-        push(kv_out.at[pp], kv_in.at[p], send.at[8], recv.at[6], (dev, x))
-
-    loop(1, np_, send_kv)
-
-    wait_recv(wo_in.at[pl.ds(0, np_ - 1)], recv.at[5])
+    push(kc_out.at[1 - c], kc_in, send.at[9], recv.at[6], (twin, x))
+
+    wait_recv(kc_in, recv.at[6])
+
+    def sum_kc(yy):
+        for j in range(2):
+            ky_out[yy, j] = (kc_out[c, j, yy].astype(F32) + kc_in[j, yy].astype(F32)).astype(BF16)
+
+    loop(0, ny, sum_kc)
+    ky_in[y] = ky_out[y]
+
+    def send_ky(k):
+        yy, dev = y_peer(k)
+        push(ky_out.at[yy], ky_in.at[y], send.at[10], recv.at[9], (dev, x))
+
+    loop(1, ny, send_ky)
+
+    wait_recv(wo_in.at[pl.ds(0, ny - 1)], recv.at[5])
 
     def sum_wo(i):
         acc = wo_in[0, i].astype(F32)
-        for j in range(1, np_):
+        for j in range(1, ny):
             acc = acc + wo_in[j, i].astype(F32)
         wz_out[i] = acc.astype(BF16)
 
@@ -355,7 +423,7 @@
 
     def send_wz(k):
         zz, dev = t_peer(k)
-        push(wz_out.at[zz], wz_in.at[z], send.at[9], recv.at[7], (dev, y))
+        push(wz_out.at[zz], wz_in.at[z], send.at[11], recv.at[7], (dev, y))
 
     @pl.when(x != y)
     def _():
@@ -367,13 +435,13 @@
 
     loop(1, nz, send_wz)
 
-    wait_recv(kv_in.at[pl.ds(0, np_ - 1)], recv.at[6])
+    wait_recv(ky_in.at[pl.ds(0, ny - 1)], recv.at[9])
     rows = 2 * halves * kr
     acc = None
     for j in range(2):
-        tot = kv_in[0, j].astype(F32)
-        for i in range(1, np_):
-            tot = tot + kv_in[i, j].astype(F32)
+        tot = ky_in[0, j].astype(F32)
+        for i in range(1, ny):
+            tot = tot + ky_in[i, j].astype(F32)
         tot = tot.astype(BF16)
         for h in range(halves):
             r, s = iota((nz * rows, nz * kr), 0), iota((nz * rows, nz * kr), 1)
@@ -390,7 +458,7 @@
 
     def send_kz(k):
         zz, dev = z_peer(k)
-        push(kz_out.at[zz], kz_in.at[z], send.at[10], recv.at[8], (dev, x))
+        push(kz_out.at[zz], kz_in.at[z], send.at[12], recv.at[8], (dev, x))
 
     loop(1, nz, send_kz)
 
@@ -418,23 +486,37 @@
 
     wait_send(mout_a.at[pl.ds(0, nz - 1)], send.at[0])
     wait_send(out_a.at[:, pl.ds(0, nz - 1)], send.at[1])
-    wait_send(wall.at[pl.ds(0, nx - 1)], send.at[2])
+    wait_send(aall, send.at[2])
     wait_send(aall.at[pl.ds(0, nx - 1)], send.at[3])
     wait_send(min_b.at[pl.ds(0, np_ - 1)], send.at[4])
     wait_send(out_b.at[:, pl.ds(0, np_ - 1)], send.at[5])
-    wait_send(ga_out.at[pl.ds(0, nx - 1)], send.at[6])
-    wait_send(wo_out.at[pl.ds(0, np_ - 1)], send.at[7])
-    wait_send(kv_out.at[pl.ds(0, np_ - 1)], send.at[8])
+    wait_send(bgx.at[:, pl.ds(0, nx - 1)], send.at[6])
+    wait_send(bgt_in, send.at[7])
+    wait_send(wo_out.at[pl.ds(0, ny - 1)], send.at[8])
+    wait_send(kc_in, send.at[9])
+    wait_send(ky_out.at[pl.ds(0, ny - 1)], send.at[10])
 
     @pl.when(x != y)
     def _():
-        wait_send(wz_out, send.at[9])
+        wait_send(wz_out, send.at[11])
 
     @pl.when(x == y)
     def _():
-        wait_send(wz_out.at[pl.ds(0, nz - 1)], send.at[9])
-
-    wait_send(kz_out.at[pl.ds(0, nz - 1)], send.at[10])
+        wait_send(wz_out.at[pl.ds(0, nz - 1)], send.at[11])
+
+    wait_send(kz_out.at[pl.ds(0, nz - 1)], send.at[12])
+
+
+def store(*refs):
+    count = (len(refs) - 1) // 2
+    done = refs[-1]
+    copies = [
+        pltpu.make_async_copy(refs[i], refs[count + i], done.at[i]) for i in range(count)
+    ]
+    for copy in copies:
+        copy.start()
+    for copy in copies:
+        copy.wait()
 
 
 def body(face_grads, face_owner, face_slot, queries, keys, values, w_out, branch_gate):
@@ -459,15 +541,16 @@
     vmem = pltpu.VMEM
     dma = pltpu.SemaphoreType.DMA
     spec = pl.BlockSpec(memory_space=pltpu.VMEM)
-    return pl.pallas_call(
+    outs = (
+        jax.ShapeDtypeStruct((tok, hw), BF16),
+        jax.ShapeDtypeStruct((rw, hw), F32),
+        jax.ShapeDtypeStruct((kr, hw), F32),
+        jax.ShapeDtypeStruct((kr, hw), F32),
+    )
+    results = pl.pallas_call(
         functools.partial(kernel, nx, nz),
-        out_shape=(
-            jax.ShapeDtypeStruct((tok, hw), BF16),
-            jax.ShapeDtypeStruct((rw, hw), F32),
-            jax.ShapeDtypeStruct((kr, hw), F32),
-            jax.ShapeDtypeStruct((kr, hw), F32),
-        ),
-        in_specs=[spec] * 8,
+        out_shape=outs,
+        in_specs=[pl.BlockSpec(memory_space=pltpu.HBM)] * 8,
         out_specs=(spec,) * 4,
         scratch_shapes=[
             vmem((ch, nz, ma, LANES), BF16),
@@ -478,42 +561,68 @@
             vmem((np_, nz, lanes_m), F32),
             vmem((ch, np_, nz * cap, LANES), BF16),
             vmem((ch, np_, nz * cap, LANES), BF16),
-            vmem((nx, hw, dx), BF16),
             vmem((nx, tok, hw), BF16),
             vmem((nx, tok, hw), BF16),
-            vmem((nx, tok, hw), BF16),
-            vmem((np_, nz, rw, hw), BF16),
-            vmem((np_, nz, rw, hw), BF16),
+            vmem((ch, nx, tok, LANES), BF16),
+            vmem((CORES, nz * rw, tok), BF16),
+            vmem((nz * rw, tok), BF16),
+            vmem((ny, nz, rw, hw), BF16),
+            vmem((ny, nz, rw, hw), BF16),
             vmem((nz, rw, hw), BF16),
             vmem((nz, rw, hw), BF16),
-            vmem((np_, 2, nz * kr, hw), BF16),
-            vmem((np_, 2, nz * kr, hw), BF16),
+            vmem((CORES, 2, ny, nz * kr, hw), BF16),
+            vmem((2, ny, nz * kr, hw), BF16),
+            vmem((ny, 2, nz * kr, hw), BF16),
+            vmem((ny, 2, nz * kr, hw), BF16),
             vmem((nz, rows, LANES), BF16),
             vmem((nz, rows, LANES), BF16),
             vmem((heads, tok, ctx), F32),
             vmem((heads, tok, ctx), BF16),
             vmem((ctx, hw), BF16),
             vmem((ctx, hw), BF16),
-            vmem((tok, dx), BF16),
+            vmem((tok, hw), F32),
             vmem((places, places), BF16),
-            dma((11,)),
+            vmem((dx, dx), BF16),
+            vmem((hw, width), BF16),
+            vmem((faces, dx), BF16),
+            vmem((1, faces), jnp.int32),
+            vmem((1, faces), jnp.int32),
+            vmem((tok, hw), BF16),
+            vmem((ctx, hw), BF16),
+            vmem((ctx, hw), BF16),
+            vmem((1, width), F32),
+            dma((8,)),
+            dma((13,)),
             dma((ch,)),
             dma((ch,)),
-            dma((9,)),
+            dma((ch,)),
+            dma((10,)),
         ],
         compiler_params=pltpu.CompilerParams(
-            collective_id=0, has_side_effects=True, vmem_limit_bytes=44 << 20
+            collective_id=0, has_side_effects=True, vmem_limit_bytes=24 << 20
         ),
     )(
-        face_grads,
-        face_owner.reshape(1, faces),
-        face_slot.reshape(1, faces),
-        queries,
-        keys,
-        values,
-        w_out,
-        branch_gate.reshape(1, width),
+        *[
+            pltpu.with_memory_space_constraint(a, pltpu.HBM)
+            for a in (
+                face_grads,
+                face_owner.reshape(1, faces),
+                face_slot.reshape(1, faces),
+                queries,
+                keys,
+                values,
+                w_out,
+                branch_gate.reshape(1, width),
+            )
+        ]
     )
+    return pl.pallas_call(
+        store,
+        out_shape=outs,
+        in_specs=[spec] * 4,
+        out_specs=(pl.BlockSpec(memory_space=pltpu.HBM),) * 4,
+        scratch_shapes=[dma((4,))],
+    )(*[pltpu.with_memory_space_constraint(r, pltpu.VMEM) for r in results])
 
 
 def solution(mesh):

time: 96.5 us -> 80.1 us (0.83)
  the two profiles are of different devices: /device:TPU:5 before, /device:TPU:1 now
where the time goes in v2:
time: 80.1 us; the launch traced here: 79.9 us
  Pallas kernels  79.3 us (99%)
    pallas_call x1, Pallas kernels, body(): pl.pallas_call(functools.partial(kernel, nx, nz), out_shape=outs, in_spec...  78.6 us

profile of v2, /device:TPU:1, one launch (start us, length us, event | category | flops | bytes accessed | tf_op | source)
XLA Modules:
  0.0 79.9 jit_solution(11194746246334221389)
XLA Ops:
  0.6 78.6 %shard_map.111 = (bf16[256,256]{1,0:T(8,128)(2,1)S(1)}, f32[16,256]{1,0:T(8,128)S(1)}, f32[4,256]{1,0:T(4,128)S(1)}, f32[4,256]{1,0:T(4,128)S(1)}) custom-call(bf16[256,512]{1,0:T(8,128)(2,1)} %face_hbm.1, s32[1,256]{1,0:T(1,128)} %bitcast.4, s32[1,256]{1,0:T(1,128)} %bitcast.5, bf16[256,256]{1,0:T(8,128)(2,1)} %q_hbm.1, bf16[512,256]{1,0:T(8,128)(2,1)} %k_hbm.1, ...), custom_call_target="tpu_custom_call" | custom-call | tf_op jit(solution)/shard_map/pallas_call | solution.py:550
  79.2 0.7 shard_map.112

commit v3 on v2

--- a/solution.py
+++ b/solution.py
@@ -10,6 +10,7 @@
 
 HD = 128
 LANES = 128
+AHEAD = 3
 CORES = 2
 MESH = pl.DeviceIdType.MESH
 F32 = jnp.float32
@@ -70,6 +71,8 @@
     wo_in,
     wz_out,
     wz_in,
+    wf_out,
+    wf_in,
     kc_out,
     kc_in,
     ky_out,
@@ -96,6 +99,10 @@
     recv_a,
     recv_b,
     recv_x,
+    recv_t,
+    recv_w,
+    recv_c,
+    recv_y,
     recv,
 ):
     loads = [
@@ -113,9 +120,6 @@
             )
         )
     ]
-    for copy in loads:
-        copy.start()
-
     ny = nx
     np_ = ny * CORES
     ch, _, ma, _ = out_a.shape
@@ -151,9 +155,7 @@
         yy = lax.rem(y + k, ny)
         return yy, (yy * nz + z) * CORES + c
 
-    def t_peer(k):
-        zz = lax.rem(z + k, nz)
-        return zz, (x * nz + zz) * CORES + c
+    mirror = ((x * nz + z) * CORES + c, y)
 
     def loop(lo, hi, f):
         def step(i, carry):
@@ -162,6 +164,14 @@
 
         lax.fori_loop(lo, hi, step, 0)
 
+    def far_first(f):
+        half = nz // 2
+
+        def step(j):
+            f(jnp.where(lax.rem(j, 2) == 0, half + lax.div(j, 2), half - lax.div(j + 1, 2)))
+
+        loop(0, nz - 1, step)
+
     def push(src, dst, ssem, rsem, dev):
         pltpu.make_async_remote_copy(
             src_ref=src, dst_ref=dst, send_sem=ssem, recv_sem=rsem, device_id=dev, device_id_type=MESH
@@ -182,13 +192,18 @@
     def greet(dev):
         pl.semaphore_signal(barrier, inc=1, device_id=dev, device_id_type=MESH)
 
-    loop(1, nz, lambda k: greet((z_peer(k)[1], x)))
+    far_first(lambda k: greet((z_peer(k)[1], x)))
+    for copy in loads[:3]:
+        copy.start()
     loop(1, np_, lambda k: greet((p_peer(k)[1], x)))
     loop(1, nx, lambda k: greet((d, lax.rem(x + k, nx))))
 
     @pl.when(x != y)
     def _():
-        loop(0, nz, lambda k: greet((t_peer(k)[1], y)))
+        greet(mirror)
+
+    for copy in loads[3:]:
+        copy.start()
 
     loads[0].wait()
     loads[1].wait()
@@ -224,26 +239,27 @@
 
     loads[2].wait()
     fill(0)
-    pl.semaphore_wait(barrier, (nz - 1) + (np_ - 1) + (nx - 1) + jnp.where(x == y, 0, nz))
+    pl.semaphore_wait(barrier, (nz - 1) + (np_ - 1) + (nx - 1) + jnp.where(x == y, 0, 1))
 
     def send_meta(k):
         zz, dev = z_peer(k)
         push(mout_a.at[zz], min_a.at[z], send.at[0], recv.at[0], (dev, x))
 
-    loop(1, nz, send_meta)
+    far_first(send_meta)
 
     def send_a(i):
         def step(k):
             zz, dev = z_peer(k)
             push(out_a.at[i, zz], in_a.at[i, z], send.at[1], recv_a.at[i], (dev, x))
 
-        loop(1, nz, step)
+        far_first(step)
 
     send_a(0)
 
     for i in range(1, ch):
         fill(i)
-        send_a(i)
+        if i < AHEAD:
+            send_a(i)
     for copy in loads[3:]:
         copy.wait()
 
@@ -258,14 +274,14 @@
     vp[...] = dot(perm_k, v_ref[...]).astype(BF16)
     for h in range(heads):
         cols = slice(h * HD, (h + 1) * HD)
-        scores = dot(q_ref[:, cols], kp[:, cols], NT) * scale
-        top = jnp.max(scores, axis=-1, keepdims=True)
+        scores = dot(kp[:, cols], q_ref[:, cols], NT) * scale
+        top = jnp.max(scores, axis=0, keepdims=True)
         e = jnp.exp(scores - top)
-        w = e / jnp.sum(e, axis=-1, keepdims=True)
+        w = e / jnp.sum(e, axis=0, keepdims=True)
         wts[h] = w
         pb = w.astype(BF16)
         probs[h] = pb
-        aall[x, :, cols] = dot(pb, vp[:, cols]).astype(BF16)
+        aall[x, :, cols] = dot(pb, vp[:, cols], TN).astype(BF16)
 
     def send_att(k):
         xx = lax.rem(x + k, nx)
@@ -278,12 +294,13 @@
     o_p = (old >> log2(cap)) & (np_ - 1)
     o_z = old >> log2(ma)
     perm_b[...] = one_hot(new == (o_p * nz + o_z) * cap + o_r)
-    new, old = iota((dx, dx), 0), iota((dx, dx), 1)
+    new, old = iota((LANES, LANES), 0), iota((LANES, LANES), 1)
     b_r = log2(rw)
+    zc = LANES // (CORES * rw)
     o_r = old & (rw - 1)
     o_c = (old >> b_r) & (CORES - 1)
     o_z = old >> (b_r + b_c)
-    perm_w[...] = one_hot(new == (o_c * nz + o_z) * rw + o_r)
+    perm_w[...] = one_hot(new == (o_c * zc + o_z) * rw + o_r)
 
     wait_recv(min_a.at[pl.ds(0, nz - 1)], recv.at[0])
     for i in range(nz):
@@ -298,6 +315,8 @@
 
     def forward(i):
         wait_recv(in_a.at[i, pl.ds(0, nz - 1)], recv_a.at[i])
+        if i + AHEAD < ch:
+            send_a(i + AHEAD)
         moved = dot(perm_b[...], in_a[i].reshape(places, LANES)).astype(BF16)
         out_b[i] = moved.reshape(np_, nz * cap, LANES)
         in_b[i, p] = out_b[i, p]
@@ -348,102 +367,100 @@
         else:
             ga_acc[...] += part
 
+    def turn(i):
+        bgt[i] = dot(perm_w[...], bgx[i, x], NT).astype(BF16).reshape(CORES, zc * rw, tok)
+        push(bgt.at[i, 1 - c], bgt_in.at[i], send.at[7], recv_t.at[i], (twin, x))
+
+    def outer(i):
+        wait_recv(bgt_in.at[i], recv_t.at[i])
+        for yy in range(ny):
+            part = dot(bgt[i, c], aall[yy]) + dot(bgt_in[i], asib[yy])
+            wo_out[i, yy] = part.astype(BF16).reshape(zc, rw, hw)
+        wo_in[i, y] = wo_out[i, y]
+
+        def step(k):
+            yy, dev = y_peer(k)
+            push(wo_out.at[i, yy], wo_in.at[i, y], send.at[8], recv_w.at[i], (dev, x))
+
+        loop(1, ny, step)
+
     landing(0)
+    turn(0)
 
     wait_recv(aall.at[pl.ds(0, nx - 1)], recv.at[2])
     push(aall, asib, send.at[2], recv.at[1], (twin, x))
 
     for i in range(1, ch):
         forward(i)
+        if i == 1:
+            wait_recv(asib, recv.at[1])
+        outer(i - 1)
         project(i - 1)
         landing(i)
-
-    turned = None
-    for i in range(ch):
-        term = dot(perm_w[:, i * LANES : (i + 1) * LANES], bgx[i, x], NT)
-        turned = term if turned is None else turned + term
-    bgt[...] = turned.astype(BF16).reshape(CORES, nz * rw, tok)
-    push(bgt.at[1 - c], bgt_in, send.at[7], recv.at[4], (twin, x))
-    wait_recv(asib, recv.at[1])
-    wait_recv(bgt_in, recv.at[4])
-
-    def outer(xx):
-        part = dot(bgt[c], aall[xx]) + dot(bgt_in[...], asib[xx])
-        wo_out[xx] = part.astype(BF16).reshape(nz, rw, hw)
-
-    loop(0, ny, outer)
-    wo_in[y] = wo_out[y]
-
-    def send_wo(k):
-        yy, dev = y_peer(k)
-        push(wo_out.at[yy], wo_in.at[y], send.at[8], recv.at[5], (dev, x))
-
-    loop(1, ny, send_wo)
-
+        turn(i)
+
+    outer(ch - 1)
     project(ch - 1)
     ga = ga_acc[...].astype(BF16)
+    score_grads = []
     for h in range(heads):
         cols = slice(h * HD, (h + 1) * HD)
         ga_h = ga[:, cols]
-        gp = dot(ga_h, vp[:, cols], NT)
+        gp = dot(vp[:, cols], ga_h, NT)
         w = wts[h]
-        delta = jnp.sum(w * gp, axis=-1, keepdims=True)
+        delta = jnp.sum(w * gp, axis=0, keepdims=True)
         sg = (w * (gp - delta)).astype(BF16)
-        gk_h = (scale * dot(sg, q_ref[:, cols], TN)).astype(BF16)
-        gv_h = dot(probs[h], ga_h, TN).astype(BF16)
-        kc_out[:, 0, :, :, cols] = gk_h.reshape(CORES, ny, nz * kr, HD)
-        kc_out[:, 1, :, :, cols] = gv_h.reshape(CORES, ny, nz * kr, HD)
-        gq_ref[:, cols] = (scale * dot(sg, kp[:, cols])).astype(BF16)
-    push(kc_out.at[1 - c], kc_in, send.at[9], recv.at[6], (twin, x))
-
-    wait_recv(kc_in, recv.at[6])
-
-    def sum_kc(yy):
-        for j in range(2):
-            ky_out[yy, j] = (kc_out[c, j, yy].astype(F32) + kc_in[j, yy].astype(F32)).astype(BF16)
-
-    loop(0, ny, sum_kc)
-    ky_in[y] = ky_out[y]
-
-    def send_ky(k):
-        yy, dev = y_peer(k)
-        push(ky_out.at[yy], ky_in.at[y], send.at[10], recv.at[9], (dev, x))
-
-    loop(1, ny, send_ky)
-
-    wait_recv(wo_in.at[pl.ds(0, ny - 1)], recv.at[5])
+        score_grads.append(sg)
+        gk_h = (scale * dot(sg, q_ref[:, cols])).astype(BF16)
+        gv_h = dot(probs[h], ga_h).astype(BF16)
+        kc_out[h, :, 0] = gk_h.reshape(CORES, ny, nz * kr, HD)
+        kc_out[h, :, 1] = gv_h.reshape(CORES, ny, nz * kr, HD)
+        push(kc_out.at[h, 1 - c], kc_in.at[h], send.at[9], recv_c.at[h], (twin, x))
 
     def sum_wo(i):
-        acc = wo_in[0, i].astype(F32)
-        for j in range(1, ny):
-            acc = acc + wo_in[j, i].astype(F32)
-        wz_out[i] = acc.astype(BF16)
-
-    loop(0, nz, sum_wo)
+        wait_recv(wo_in.at[i, pl.ds(0, ny - 1)], recv_w.at[i])
+
+        def step(k):
+            acc = wo_in[i, 0, k].astype(F32)
+            for j in range(1, ny):
+                acc = acc + wo_in[i, j, k].astype(F32)
+            wz_out[i * zc + k] = acc.astype(BF16)
+
+        loop(0, zc, step)
+
+    for i in range(ch):
+        sum_wo(i)
+    wz_in[z] = wz_out[z]
 
     def send_wz(k):
-        zz, dev = t_peer(k)
-        push(wz_out.at[zz], wz_in.at[z], send.at[11], recv.at[7], (dev, y))
-
-    @pl.when(x != y)
-    def _():
-        send_wz(0)
-
-    @pl.when(x == y)
-    def _():
-        wz_in[z] = wz_out[z]
-
-    loop(1, nz, send_wz)
-
-    wait_recv(ky_in.at[pl.ds(0, ny - 1)], recv.at[9])
+        zz, dev = z_peer(k)
+        push(wz_out.at[zz], wz_in.at[z], send.at[11], recv.at[7], (dev, x))
+
+    far_first(send_wz)
+
+    for h in range(heads):
+        wait_recv(kc_in.at[h], recv_c.at[h])
+        for yy in range(ny):
+            for j in range(2):
+                ky_out[h, yy, j] = (
+                    kc_out[h, c, j, yy].astype(F32) + kc_in[h, j, yy].astype(F32)
+                ).astype(BF16)
+        ky_in[h, y] = ky_out[h, y]
+
+        def send_ky(k, h=h):
+            yy, dev = y_peer(k)
+            push(ky_out.at[h, yy], ky_in.at[h, y], send.at[10], recv_y.at[h], (dev, x))
+
+        loop(1, ny, send_ky)
+
     rows = 2 * halves * kr
     acc = None
-    for j in range(2):
-        tot = ky_in[0, j].astype(F32)
-        for i in range(1, ny):
-            tot = tot + ky_in[i, j].astype(F32)
-        tot = tot.astype(BF16)
-        for h in range(halves):
+    for h in range(heads):
+        wait_recv(ky_in.at[h, pl.ds(0, ny - 1)], recv_y.at[h])
+        for j in range(2):
+            tot = ky_in[h, 0, j].astype(F32)
+            for i in range(1, ny):
+                tot = tot + ky_in[h, i, j].astype(F32)
             r, s = iota((nz * rows, nz * kr), 0), iota((nz * rows, nz * kr), 1)
             inner = r & (rows - 1)
             sel = (
@@ -451,7 +468,7 @@
                 & ((inner >> b_k) == j * halves + h)
                 & ((inner & (kr - 1)) == (s & (kr - 1)))
             )
-            part = dot(one_hot(sel), tot[:, h * LANES : (h + 1) * LANES])
+            part = dot(one_hot(sel), tot.astype(BF16))
             acc = part if acc is None else acc + part
     kz_out[...] = acc.astype(BF16).reshape(nz, rows, LANES)
     kz_in[z] = kz_out[z]
@@ -460,20 +477,25 @@
         zz, dev = z_peer(k)
         push(kz_out.at[zz], kz_in.at[z], send.at[12], recv.at[8], (dev, x))
 
-    loop(1, nz, send_kz)
-
-    @pl.when(x != y)
-    def _():
-        wait_recv(wz_in, recv.at[7])
-
-    @pl.when(x == y)
-    def _():
-        wait_recv(wz_in.at[pl.ds(0, nz - 1)], recv.at[7])
-
+    far_first(send_kz)
+
+    wait_recv(wz_in.at[pl.ds(0, nz - 1)], recv.at[7])
     acc = wz_in[0].astype(F32)
     for i in range(1, nz):
         acc = acc + wz_in[i].astype(F32)
-    gwo_ref[...] = acc
+    wf_out[...] = acc
+
+    @pl.when(x != y)
+    def _():
+        push(wf_out, wf_in, send.at[13], recv.at[6], mirror)
+
+    @pl.when(x == y)
+    def _():
+        wf_in[...] = wf_out[...]
+
+    for h in range(heads):
+        cols = slice(h * HD, (h + 1) * HD)
+        gq_ref[:, cols] = (scale * dot(score_grads[h], kp[:, cols], TN)).astype(BF16)
 
     wait_recv(kz_in.at[pl.ds(0, nz - 1)], recv.at[8])
     acc = kz_in[0].astype(F32)
@@ -484,6 +506,12 @@
         gk_ref[:, cols] = acc[h * kr : (h + 1) * kr, :]
         gv_ref[:, cols] = acc[(halves + h) * kr : (halves + h + 1) * kr, :]
 
+    @pl.when(x != y)
+    def _():
+        wait_recv(wf_in, recv.at[6])
+
+    gwo_ref[...] = wf_in[...]
+
     wait_send(mout_a.at[pl.ds(0, nz - 1)], send.at[0])
     wait_send(out_a.at[:, pl.ds(0, nz - 1)], send.at[1])
     wait_send(aall, send.at[2])
@@ -492,17 +520,15 @@
     wait_send(out_b.at[:, pl.ds(0, np_ - 1)], send.at[5])
     wait_send(bgx.at[:, pl.ds(0, nx - 1)], send.at[6])
     wait_send(bgt_in, send.at[7])
-    wait_send(wo_out.at[pl.ds(0, ny - 1)], send.at[8])
+    wait_send(wo_out.at[:, pl.ds(0, ny - 1)], send.at[8])
     wait_send(kc_in, send.at[9])
-    wait_send(ky_out.at[pl.ds(0, ny - 1)], send.at[10])
+    wait_send(ky_out.at[:, pl.ds(0, ny - 1)], send.at[10])
+
+    wait_send(wz_out.at[pl.ds(0, nz - 1)], send.at[11])
 
     @pl.when(x != y)
     def _():
-        wait_send(wz_out, send.at[11])
-
-    @pl.when(x == y)
-    def _():
-        wait_send(wz_out.at[pl.ds(0, nz - 1)], send.at[11])
+        wait_send(wf_out, send.at[13])
 
     wait_send(kz_out.at[pl.ds(0, nz - 1)], send.at[12])
 
@@ -564,25 +590,27 @@
             vmem((nx, tok, hw), BF16),
             vmem((nx, tok, hw), BF16),
             vmem((ch, nx, tok, LANES), BF16),
-            vmem((CORES, nz * rw, tok), BF16),
-            vmem((nz * rw, tok), BF16),
-            vmem((ny, nz, rw, hw), BF16),
-            vmem((ny, nz, rw, hw), BF16),
+            vmem((ch, CORES, LANES // CORES, tok), BF16),
+            vmem((ch, LANES // CORES, tok), BF16),
+            vmem((ch, ny, nz // ch, rw, hw), BF16),
+            vmem((ch, ny, nz // ch, rw, hw), BF16),
             vmem((nz, rw, hw), BF16),
             vmem((nz, rw, hw), BF16),
-            vmem((CORES, 2, ny, nz * kr, hw), BF16),
-            vmem((2, ny, nz * kr, hw), BF16),
-            vmem((ny, 2, nz * kr, hw), BF16),
-            vmem((ny, 2, nz * kr, hw), BF16),
+            vmem((rw, hw), F32),
+            vmem((rw, hw), F32),
+            vmem((heads, CORES, 2, ny, nz * kr, HD), BF16),
+            vmem((heads, 2, ny, nz * kr, HD), BF16),
+            vmem((heads, ny, 2, nz * kr, HD), BF16),
+            vmem((heads, ny, 2, nz * kr, HD), BF16),
             vmem((nz, rows, LANES), BF16),
             vmem((nz, rows, LANES), BF16),
-            vmem((heads, tok, ctx), F32),
-            vmem((heads, tok, ctx), BF16),
+            vmem((heads, ctx, tok), F32),
+            vmem((heads, ctx, tok), BF16),
             vmem((ctx, hw), BF16),
             vmem((ctx, hw), BF16),
             vmem((tok, hw), F32),
             vmem((places, places), BF16),
-            vmem((dx, dx), BF16),
+            vmem((LANES, LANES), BF16),
             vmem((hw, width), BF16),
             vmem((faces, dx), BF16),
             vmem((1, faces), jnp.int32),
@@ -592,10 +620,14 @@
             vmem((ctx, hw), BF16),
             vmem((1, width), F32),
             dma((8,)),
-            dma((13,)),
+            dma((14,)),
             dma((ch,)),
             dma((ch,)),
             dma((ch,)),
+            dma((ch,)),
+            dma((ch,)),
+            dma((heads,)),
+            dma((heads,)),
             dma((10,)),
         ],
         compiler_params=pltpu.CompilerParams(

time: 80.1 us -> 72.5 us (0.905)
  Pallas kernels: 79.3 us -> 71.7 us
    pallas_call x1, Pallas kernels: 78.6 us -> 71 us  [body(): pl.pallas_call(functools.partial(kernel, nx, nz), out_shape=outs, in_spec...]
where the time goes in v3:
time: 72.5 us; the launch traced here: 72.3 us
  Pallas kernels  71.7 us (99%)
    pallas_call x1, Pallas kernels, body(): pl.pallas_call(functools.partial(kernel, nx, nz), out_shape=outs, in_spec...  71 us

profile of v3, /device:TPU:1, one launch (start us, length us, event | category | flops | bytes accessed | tf_op | source)
XLA Modules:
  0.0 72.3 jit_solution(7939442922636409043)
XLA Ops:
  0.6 71.0 %shard_map.111 = (bf16[256,256]{1,0:T(8,128)(2,1)S(1)}, f32[16,256]{1,0:T(8,128)S(1)}, f32[4,256]{1,0:T(4,128)S(1)}, f32[4,256]{1,0:T(4,128)S(1)}) custom-call(bf16[256,512]{1,0:T(8,128)(2,1)} %face_hbm.1, s32[1,256]{1,0:T(1,128)} %bitcast.4, s32[1,256]{1,0:T(1,128)} %bitcast.5, bf16[256,256]{1,0:T(8,128)(2,1)} %q_hbm.1, bf16[512,256]{1,0:T(8,128)(2,1)} %k_hbm.1, ...), custom_call_target="tpu_custom_call" | custom-call | tf_op jit(solution)/shard_map/pallas_call | solution.py:576
  71.6 0.7 shard_map.112

commit v4 on v3

--- a/solution.py
+++ b/solution.py
@@ -10,7 +10,7 @@
 
 HD = 128
 LANES = 128
-AHEAD = 3
+AHEAD = 2
 CORES = 2
 MESH = pl.DeviceIdType.MESH
 F32 = jnp.float32
@@ -86,6 +86,7 @@
     ga_acc,
     perm_b,
     perm_w,
+    perm_k,
     w_ref,
     face_ref,
     owner_ref,
@@ -269,9 +270,9 @@
     o_c = (old >> b_k) & (CORES - 1)
     o_z = (old >> (b_k + b_c)) & (nz - 1)
     o_y = old >> (b_k + b_c + b_z)
-    perm_k = one_hot(new == ((o_c * ny + o_y) * nz + o_z) * kr + o_k)
-    kp[...] = dot(perm_k, k_ref[...]).astype(BF16)
-    vp[...] = dot(perm_k, v_ref[...]).astype(BF16)
+    reorder = one_hot(new == ((o_c * ny + o_y) * nz + o_z) * kr + o_k)
+    kp[...] = dot(reorder, k_ref[...]).astype(BF16)
+    vp[...] = dot(reorder, v_ref[...]).astype(BF16)
     for h in range(heads):
         cols = slice(h * HD, (h + 1) * HD)
         scores = dot(kp[:, cols], q_ref[:, cols], NT) * scale
@@ -294,6 +295,15 @@
     o_p = (old >> log2(cap)) & (np_ - 1)
     o_z = old >> log2(ma)
     perm_b[...] = one_hot(new == (o_p * nz + o_z) * cap + o_r)
+    rows = 2 * halves * kr
+    new, old = iota((nz * rows, nz * kr), 0), iota((nz * rows, nz * kr), 1)
+    inner = new & (rows - 1)
+    for i in range(2 * halves):
+        perm_k[i] = one_hot(
+            ((new >> log2(rows)) == (old >> b_k))
+            & ((inner >> b_k) == i)
+            & ((inner & (kr - 1)) == (old & (kr - 1)))
+        )
     new, old = iota((LANES, LANES), 0), iota((LANES, LANES), 1)
     b_r = log2(rw)
     zc = LANES // (CORES * rw)
@@ -321,11 +331,9 @@
         out_b[i] = moved.reshape(np_, nz * cap, LANES)
         in_b[i, p] = out_b[i, p]
 
-        def step(k):
+        for k in sorted(range(1, np_), key=lambda k: abs(k - np_ // 2)):
             pp, dev = p_peer(k)
             push(out_b.at[i, pp], in_b.at[i, p], send.at[5], recv_b.at[i], (dev, x))
-
-        loop(1, np_, step)
 
     forward(0)
 
@@ -349,23 +357,18 @@
         grad_out = dot(land, in_b[i].reshape(places, LANES)).astype(BF16)
         bgx[i, x] = (gate[:, i * LANES : (i + 1) * LANES] * grad_out.astype(F32)).astype(BF16)
 
-        def step(k):
+        for k in sorted(range(1, nx), key=lambda k: abs(k - nx // 2)):
             xx = lax.rem(x + k, nx)
             push(bgx.at[i, x], bgx.at[i, x], send.at[6], recv_x.at[i], (d, xx))
 
-        loop(1, nx, step)
-
     def project(i):
         wait_recv(bgx.at[i, pl.ds(0, nx - 1)], recv_x.at[i])
-        part = None
+        part = ga_acc[...] if i else None
         for xx in range(nx):
             first = xx * dx + i * LANES
             term = dot(bgx[i, xx], w_ref[:, first : first + LANES], NT)
             part = term if part is None else part + term
-        if i == 0:
-            ga_acc[...] = part
-        else:
-            ga_acc[...] += part
+        ga_acc[...] = part
 
     def turn(i):
         bgt[i] = dot(perm_w[...], bgx[i, x], NT).astype(BF16).reshape(CORES, zc * rw, tok)
@@ -447,13 +450,10 @@
                 ).astype(BF16)
         ky_in[h, y] = ky_out[h, y]
 
-        def send_ky(k, h=h):
+        for k in sorted(range(1, ny), key=lambda k: abs(k - ny // 2)):
             yy, dev = y_peer(k)
             push(ky_out.at[h, yy], ky_in.at[h, y], send.at[10], recv_y.at[h], (dev, x))
 
-        loop(1, ny, send_ky)
-
-    rows = 2 * halves * kr
     acc = None
     for h in range(heads):
         wait_recv(ky_in.at[h, pl.ds(0, ny - 1)], recv_y.at[h])
@@ -461,14 +461,7 @@
             tot = ky_in[h, 0, j].astype(F32)
             for i in range(1, ny):
                 tot = tot + ky_in[h, i, j].astype(F32)
-            r, s = iota((nz * rows, nz * kr), 0), iota((nz * rows, nz * kr), 1)
-            inner = r & (rows - 1)
-            sel = (
-                ((r >> log2(rows)) == (s >> b_k))
-                & ((inner >> b_k) == j * halves + h)
-                & ((inner & (kr - 1)) == (s & (kr - 1)))
-            )
-            part = dot(one_hot(sel), tot.astype(BF16))
+            part = dot(perm_k[j * halves + h], tot.astype(BF16))
             acc = part if acc is None else acc + part
     kz_out[...] = acc.astype(BF16).reshape(nz, rows, LANES)
     kz_in[z] = kz_out[z]
@@ -611,6 +604,7 @@
             vmem((tok, hw), F32),
             vmem((places, places), BF16),
             vmem((LANES, LANES), BF16),
+            vmem((2 * (hw // LANES), nz * rows, nz * kr), BF16),
             vmem((hw, width), BF16),
             vmem((faces, dx), BF16),
             vmem((1, faces), jnp.int32),

time: 72.5 us -> 71.2 us (0.982)
  Pallas kernels: 71.7 us -> 70.4 us
    pallas_call x1, Pallas kernels: 71 us -> 69.7 us  [body(): pl.pallas_call(functools.partial(kernel, nx, nz), out_shape=outs, in_spec...]
where the time goes in v4:
time: 71.2 us; the launch traced here: 71.1 us
  Pallas kernels  70.4 us (99%)
    pallas_call x1, Pallas kernels, body(): pl.pallas_call(functools.partial(kernel, nx, nz), out_shape=outs, in_spec...  69.7 us

profile of v4, /device:TPU:1, one launch (start us, length us, event | category | flops | bytes accessed | tf_op | source)
XLA Modules:
  0.0 71.1 jit_solution(11952027299509528863)
XLA Ops:
  0.6 69.7 %shard_map.111 = (bf16[256,256]{1,0:T(8,128)(2,1)S(1)}, f32[16,256]{1,0:T(8,128)S(1)}, f32[4,256]{1,0:T(4,128)S(1)}, f32[4,256]{1,0:T(4,128)S(1)}) custom-call(bf16[256,512]{1,0:T(8,128)(2,1)} %face_hbm.1, s32[1,256]{1,0:T(1,128)} %bitcast.4, s32[1,256]{1,0:T(1,128)} %bitcast.5, bf16[256,256]{1,0:T(8,128)(2,1)} %q_hbm.1, bf16[512,256]{1,0:T(8,128)(2,1)} %k_hbm.1, ...), custom_call_target="tpu_custom_call" | custom-call | tf_op jit(solution)/shard_map/pallas_call | solution.py:569
  70.4 0.7 shard_map.112

commit v5 on v4

--- a/solution.py
+++ b/solution.py
@@ -403,6 +403,27 @@
         turn(i)
 
     outer(ch - 1)
+
+    def sum_wo(i):
+        wait_recv(wo_in.at[i, pl.ds(0, ny - 1)], recv_w.at[i])
+        for k in range(zc):
+            zz = i * zc + k
+            acc = wo_in[i, 0, k].astype(F32)
+            for j in range(1, ny):
+                acc = acc + wo_in[i, j, k].astype(F32)
+            wz_out[zz] = acc.astype(BF16)
+
+            @pl.when(z != zz)
+            def _():
+                dev = (y * nz + zz) * CORES + c
+                push(wz_out.at[zz], wz_in.at[z], send.at[11], recv.at[7], (dev, x))
+
+            @pl.when(z == zz)
+            def _():
+                wz_in[z] = wz_out[zz]
+
+    for i in range(ch - 1):
+        sum_wo(i)
     project(ch - 1)
     ga = ga_acc[...].astype(BF16)
     score_grads = []
@@ -420,26 +441,7 @@
         kc_out[h, :, 1] = gv_h.reshape(CORES, ny, nz * kr, HD)
         push(kc_out.at[h, 1 - c], kc_in.at[h], send.at[9], recv_c.at[h], (twin, x))
 
-    def sum_wo(i):
-        wait_recv(wo_in.at[i, pl.ds(0, ny - 1)], recv_w.at[i])
-
-        def step(k):
-            acc = wo_in[i, 0, k].astype(F32)
-            for j in range(1, ny):
-                acc = acc + wo_in[i, j, k].astype(F32)
-            wz_out[i * zc + k] = acc.astype(BF16)
-
-        loop(0, zc, step)
-
-    for i in range(ch):
-        sum_wo(i)
-    wz_in[z] = wz_out[z]
-
-    def send_wz(k):
-        zz, dev = z_peer(k)
-        push(wz_out.at[zz], wz_in.at[z], send.at[11], recv.at[7], (dev, x))
-
-    far_first(send_wz)
+    sum_wo(ch - 1)
 
     for h in range(heads):
         wait_recv(kc_in.at[h], recv_c.at[h])

time: 71.2 us -> 71.2 us (level)
  no operation moved by 1% of the time
where the time goes in v5:
time: 71.2 us; the launch traced here: 71 us
  Pallas kernels  70.4 us (99%)
    pallas_call x1, Pallas kernels, body(): pl.pallas_call(functools.partial(kernel, nx, nz), out_shape=outs, in_spec...  69.7 us

profile of v5, /device:TPU:1, one launch (start us, length us, event | category | flops | bytes accessed | tf_op | source)
XLA Modules:
  0.0 71.0 jit_solution(335503308725732604)
XLA Ops:
  0.6 69.7 %shard_map.111 = (bf16[256,256]{1,0:T(8,128)(2,1)S(1)}, f32[16,256]{1,0:T(8,128)S(1)}, f32[4,256]{1,0:T(4,128)S(1)}, f32[4,256]{1,0:T(4,128)S(1)}) custom-call(bf16[256,512]{1,0:T(8,128)(2,1)} %face_hbm.1, s32[1,256]{1,0:T(1,128)} %bitcast.4, s32[1,256]{1,0:T(1,128)} %bitcast.5, bf16[256,256]{1,0:T(8,128)(2,1)} %q_hbm.1, bf16[512,256]{1,0:T(8,128)(2,1)} %k_hbm.1, ...), custom_call_target="tpu_custom_call" | custom-call | tf_op jit(solution)/shard_map/pallas_call | solution.py:571
  70.3 0.7 shard_map.112
